TPU v7x, 32 devices: a whole 2x2x4 slice. The times are simulated.
32 devices in a mesh: groups: 2 (over x), pairs: 8 (over z, y), mp: 2 (over core).
Axes of the slice: x: 2, y: 2, z: 4, core: 2. Of those that a mesh axis runs over, the one named last changes fastest.
Arguments:
- tokens: bfloat16 [64, 196, 768], P(('groups', 'pairs'), None, 'mp'), parts along dimension 0, may hold values from -6 to 6
- gain_query: float32 [768], replicated, may hold values from 0.25 to 1.75
- gain_context: float32 [768], replicated, may hold values from 0.25 to 1.75
- query_weight: bfloat16 [768, 768], replicated, may hold values from -1 to 1
- key_weight: bfloat16 [768, 768], replicated, may hold values from -8 to 8
- value_weight: bfloat16 [768, 768], replicated, may hold values from -0.21875 to 0.21875
- out_weight: bfloat16 [768, 768], replicated, may hold values from -0.21875 to 0.21875
- gain_head: float32 [768], replicated, may hold values from 0.25 to 1.75
- hidden_weight: bfloat16 [768, 1024], replicated, may hold values from -0.21875 to 0.21875
- hidden_bias: float32 [1024], replicated, may hold values from -3 to 3
- point_weight: bfloat16 [4, 1024], replicated, may hold values from -0.1875 to 0.1875
- view_owner: int32 [192, 1], P('groups'), parts along dimension 0, may hold values from 0 to 7; in each aligned block of 12 rows (0 to 11, 12 to 23, ...) at most 2 rows name the same one
- view_local: int32 [192], P('groups'), parts along dimension 0, may hold values from 0 to 3
- pair_count: int32 [16], P('groups'), parts along dimension 0, may hold values from 1 to 6, 24 in all
Outputs:
- joined: float32 [64, 4, 196], P(('groups', 'pairs', 'mp')), parts along dimension 0
There are 2 independent parts, one for each index of `groups`. A program takes and returns all parts, laid end to end along the dimension named above; an argument that names none is the same for every part. Nothing has to cross between parts.
Inputs may be any that keep to these rules, and one draw needn't show every extreme that they name: `view_owner`: among the 12 views of one worker no owner appears more than 2 times, and in every draw some owner appears exactly 2 times. `pair_count`: some worker has exactly 6 pairs in every draw; the counts sum to 24.
All inputs are finite; a program needn't handle non-finite values.
Results may differ from a plain program's by a relative error of at most 0.012.
The roundings to bfloat16 on the way count: a program that leaves them out, or rounds other values in their place, can miss the bound.
Values may be sent and summed in bfloat16 or wider, within the bound.
No kernel may reach another device: no remote copies, remote signals or barrier semaphores. Data moves between devices by JAX's collectives and lax.ppermute only.
A program may use at most 128 MiB of HBM per device.

v0:
```python
import math
import jax
import jax.numpy as jnp
from jax import lax
from jax.sharding import PartitionSpec as P

HEADS = 12
EPS = 1e-06


def norm_rows(rows_in, gain_vec):
    rows_in = rows_in.astype(jnp.float32)
    average = jnp.mean(rows_in, axis=-1, keepdims=True)
    centered = rows_in - average
    variance = jnp.mean(centered * centered, axis=-1, keepdims=True)
    return (centered * lax.rsqrt(variance + EPS) * gain_vec).astype(jnp.bfloat16)


def project(rows_in, weight):
    return jnp.einsum("vtd,de->vte", rows_in, weight, preferred_element_type=jnp.float32)


def attention(queries, key_rows, value_rows, head_count):
    view_count, token_count, feature_width = queries.shape
    head_size = feature_width // head_count
    split_shape = (view_count, token_count, head_count, head_size)
    scores = jnp.einsum(
        "vqhd,vkhd->vhqk",
        queries.reshape(split_shape),
        key_rows.reshape(split_shape),
        preferred_element_type=jnp.float32,
    ) / math.sqrt(head_size)
    row_max = jnp.max(scores, axis=-1, keepdims=True)
    exponent = jnp.exp(scores - row_max)
    attn_probs = (exponent / jnp.sum(exponent, axis=-1, keepdims=True)).astype(jnp.bfloat16)
    blended = jnp.einsum(
        "vhqk,vkhd->vqhd",
        attn_probs,
        value_rows.reshape(split_shape),
        preferred_element_type=jnp.float32,
    )
    return blended.astype(jnp.bfloat16).reshape(view_count, token_count, feature_width)


def point_terms(head_out):
    confidence = 1.0 + jnp.exp(head_out[:, 3:4])
    return jnp.concatenate([head_out[:, :3] * confidence, confidence], axis=1)


def per_device(
    tokens,
    gain_query,
    gain_context,
    query_weight,
    key_weight,
    value_weight,
    out_weight,
    gain_head,
    hidden_weight,
    hidden_bias,
    point_weight,
    view_owner,
    view_local,
    pair_count,
):
    worker_count = lax.axis_size("pairs")
    worker_index = lax.axis_index("pairs")
    core_index = lax.axis_index("mp")
    core_count = lax.axis_size("mp")
    image_count = tokens.shape[0]
    token_count = tokens.shape[1]
    full_width = query_weight.shape[0]
    hidden_width = hidden_weight.shape[1]
    request_count = view_local.shape[0] // worker_count
    slot_count = request_count // 2
    owners = view_owner[:, 0].reshape(worker_count, request_count)
    local_rows = view_local.reshape(worker_count, request_count)
    global_rows = owners * image_count + local_rows
    my_images = global_rows[worker_index]
    shard_rows = lax.all_gather(tokens, "pairs", axis=0, tiled=True)
    row_ids = jnp.arange(shard_rows.shape[0])
    onehot = (my_images[:, None] == row_ids[None, :]).astype(jnp.bfloat16)
    half_views = jnp.einsum(
        "vi,itd->vtd", onehot, shard_rows, preferred_element_type=jnp.float32
    ).astype(jnp.bfloat16)
    full_views = lax.all_gather(half_views, "mp", axis=2, tiled=True)
    pair_total = pair_count[worker_index]
    part_width = full_width // core_count
    hidden_part = hidden_width // core_count
    context_views = full_views.reshape(slot_count, 2, token_count, full_width)[:, ::-1].reshape(
        request_count, token_count, full_width
    )
    query_in = norm_rows(full_views, gain_query)
    context_in = norm_rows(context_views, gain_context)
    query_part = lax.dynamic_slice_in_dim(query_weight, core_index * part_width, part_width, 1)
    key_part = lax.dynamic_slice_in_dim(key_weight, core_index * part_width, part_width, 1)
    value_part = lax.dynamic_slice_in_dim(value_weight, core_index * part_width, part_width, 1)
    query_proj = project(query_in, query_part).astype(jnp.bfloat16)
    key_proj = project(context_in, key_part).astype(jnp.bfloat16)
    value_proj = project(context_in, value_part).astype(jnp.bfloat16)
    attended_part = attention(query_proj, key_proj, value_proj, HEADS // core_count)
    attended = lax.all_gather(attended_part, "mp", axis=2, tiled=True)
    updated = full_views.astype(jnp.float32) + project(attended, out_weight)
    head_in = norm_rows(updated, gain_head)
    first_part = lax.dynamic_slice_in_dim(hidden_weight, core_index * hidden_part, hidden_part, 1)
    bias_part = lax.dynamic_slice_in_dim(hidden_bias, core_index * hidden_part, hidden_part, 0)
    second_part = lax.dynamic_slice_in_dim(point_weight, core_index * hidden_part, hidden_part, 1)
    hidden = jax.nn.gelu(project(head_in, first_part) + bias_part).astype(jnp.bfloat16)
    head_part = jnp.einsum("vth,ch->vct", hidden, second_part, preferred_element_type=jnp.float32)
    head_out = lax.psum(head_part, "mp")
    view_ids = jnp.arange(request_count)
    live_mask = jnp.logical_and(view_ids % 2 == core_index, view_ids // 2 < pair_total).astype(
        jnp.float32
    )
    contrib = point_terms(head_out) * live_mask[:, None, None]
    image_rows = my_images[view_ids]
    row_ids = jnp.arange(image_count // core_count * lax.axis_size(("pairs", "mp")))
    onehot = (image_rows[:, None] == row_ids[None, :]).astype(jnp.float32)
    return lax.psum_scatter(
        jnp.einsum("vr,vct->rct", onehot, contrib, precision=lax.Precision.HIGHEST),
        ("pairs", "mp"),
        scatter_dimension=0,
        tiled=True,
    )


def solution(mesh):
    return jax.shard_map(
        per_device,
        mesh=mesh,
        in_specs=(
            P(("groups", "pairs"), None, "mp"),
            P(),
            P(),
            P(),
            P(),
            P(),
            P(),
            P(),
            P(),
            P(),
            P(),
            P("groups", None),
            P("groups"),
            P("groups"),
        ),
        out_specs=P(("groups", "pairs", "mp"), None, None),
        check_vma=False,
    )
```

profile of v0, /device:TPU:8, one launch (start us, length us, event | category | flops | bytes accessed | tf_op | source)
XLA Modules:
  0.0 323.9 jit_solution(13960240500838489043)
XLA Ops:
  10.2 81.8 %all-gather.4.cloned.1.call-done = bf16[32,196,384]{2,1,0:T(8,128)(2,1)} async-done(((bf16[4,196,384]{2,1,0:T(8,128)(2,1)}), bf16[32,196,384]{2,1,0:T(8,128)(2,1)}) %all-gather.4.cloned.1.call-update) | async-done | bytes 4816912 | tf_op jit(solution)/shard_map/all_gather | solution.py:80
  92.0 4.7 %fusion.31 = bf16[12,196,384]{2,0,1:T(8,128)(2,1)} fusion(bf16[32,196,384]{2,1,0:T(8,128)(2,1)} %all-gather.4.cloned.1.call-done, s32[12]{0:T(128)S(1)} %fusion.77), kind=kOutput, calls=%fused_computation.41 | convolution fusion | flops 58706304 | bytes 6623280 | tf_op jit(solution)/shard_map/vi,itd->vtd/dot_general | solution.py:83
  96.8 14.0 %all-gather.6.cloned.1.call-done = bf16[12,196,768]{2,0,1:T(8,128)(2,1)} async-done(((bf16[12,196,384]{2,0,1:T(8,128)(2,1)}), bf16[12,196,768]{2,0,1:T(8,128)(2,1)}) %all-gather.6.cloned.1.call-update) | async-done | bytes 3612688 | tf_op jit(solution)/shard_map/all_gather | solution.py:86
  110.8 3.5 %copy.41 = bf16[12,196,768]{2,1,0:T(8,128)(2,1)S(1)} copy(bf16[12,196,768]{2,0,1:T(8,128)(2,1)} %all-gather.6.cloned.1.call-done) | data formatting | bytes 7225344 | tf_op jit(solution)/shard_map/all_gather | solution.py:86
  117.5 3.2 convert_reduce_fusion
  120.7 4.1 %fusion.6 = f32[12,196]{0,1:T(8,128)S(1)} fusion(bf16[12,196,768]{2,0,1:T(8,128)(2,1)} %all-gather.6.cloned.1.call-done, f32[12,196]{0,1:T(8,128)S(1)} %broadcast_multiply_fusion.1), kind=kLoop, calls=%fused_computation.11 | loop fusion | flops 7222992 | bytes 3631488 | tf_op jit(solution)/shard_map/reduce_sum | solution.py:15
  125.5 2.8 fusion.11
  128.3 3.3 %convolution_convert_fusion = bf16[12,196,384]{2,1,0:T(8,128)(2,1)S(1)} fusion(bf16[12,196,768]{2,1,0:T(8,128)(2,1)S(1)} %fusion.11, bf16[768,768]{1,0:T(8,128)(2,1)} %param.18, s32[]{:T(128)S(6)} %select_n.37), kind=kOutput, calls=%fused_computation.44 | convolution fusion | flops 1388169216 | bytes 6008836 | tf_op jit(solution)/shard_map/vtd,de->vte/dot_general | solution.py:20
  131.7 3.4 %convolution_convert_fusion.1 = bf16[12,196,384]{2,1,0:T(8,128)(2,1)} fusion(bf16[12,196,768]{2,1,0:T(8,128)(2,1)S(1)} %fusion.11, bf16[768,768]{1,0:T(8,128)(2,1)S(1)} %copy-done.6, s32[]{:T(128)S(6)} %select_n.37), kind=kOutput, calls=%fused_computation.45 | convolution fusion | flops 1388169216 | bytes 6082564 | tf_op jit(solution)/shard_map/vtd,de->vte/dot_general | solution.py:20
  135.1 4.0 %copy.42 = bf16[12,196,384]{1,2,0:T(8,128)(2,1)} copy(bf16[12,196,384]{2,1,0:T(8,128)(2,1)} %convolution_convert_fusion.1) | data formatting | bytes 3612672 | tf_op jit(solution)/shard_map/convert_element_type | solution.py:100
  141.6 4.3 %fusion.8 = bf16[12,196,768]{2,0,1:T(8,128)(2,1)S(1)} fusion(bf16[12,196,768]{2,0,1:T(8,128)(2,1)} %all-gather.6.cloned.1.call-done, f32[768]{0:T(1024)S(1)} %copy-done.3, f32[12,196]{0,1:T(8,128)} %add_rsqrt_fusion.1, f32[12,196]{0,1:T(8,128)S(1)} %broadcast_multiply_fusion.1), kind=kLoop, calls=%fused_computation.13 | loop fusion | flops 9031680 | bytes 7247232 | tf_op jit(solution)/shard_map/convert_element_type | solution.py:16
  145.9 2.9 fusion.35
  148.9 2.5 copy.44
  151.4 13.0 %fusion.83 = (f32[12,6,196]{2,1,0:T(8,128)S(1)}, f32[12,6,196,196]{2,3,1,0:T(8,128)}) fusion(bf16[12,196,6,64]{1,3,2,0:T(8,128)(2,1)} %bitcast.64, bf16[12,196,6,64]{1,3,2,0:T(8,128)(2,1)} %bitcast.63), kind=kOutput, calls=%fused_computation.98 | convolution fusion | flops 362339904 | bytes 14732928 | tf_op jit(solution)/shard_map/sub | solution.py:34
  164.4 8.9 %fusion.34 = bf16[12,6,64,196]{3,2,1,0:T(8,128)(2,1)} fusion(bf16[12,196,6,64]{1,3,2,0:T(8,128)(2,1)} %bitcast.62, f32[12,6,196,196]{2,3,1,0:T(8,128)} %get-tuple-element.6, f32[12,6,196]{2,1,0:T(8,128)S(1)} %get-tuple-element.5), kind=kOutput, calls=%fused_computation.42 | convolution fusion | flops 360476928 | bytes 14732928 | tf_op jit(solution)/shard_map/vhqk,vkhd->vqhd/dot_general | solution.py:36
  173.3 4.2 %copy.47 = bf16[12,196,384]{2,1,0:T(8,128)(2,1)} copy(bf16[12,196,384]{1,2,0:T(8,128)(2,1)} %bitcast.65) | data formatting | bytes 3612672 | tf_op jit(solution)/shard_map/reshape | solution.py:42
  179.6 12.1 %all-gather.8.cloned.1.call-done = bf16[12,196,768]{2,1,0:T(8,128)(2,1)} async-done(((bf16[12,196,384]{2,1,0:T(8,128)(2,1)}), bf16[12,196,768]{2,1,0:T(8,128)(2,1)}) %all-gather.8.cloned.1.call-update) | async-done | bytes 3612688 | tf_op jit(solution)/shard_map/all_gather | solution.py:102
  191.7 5.2 %fusion.44 = f32[12,196,768]{2,1,0:T(8,128)S(1)} fusion(bf16[12,196,768]{2,1,0:T(8,128)(2,1)} %all-gather.8.cloned.1.call-done, bf16[768,768]{1,0:T(8,128)(2,1)S(1)} %copy-done.8), kind=kOutput, calls=%fused_computation.47 | convolution fusion | flops 2774532096 | bytes 12017664 | tf_op jit(solution)/shard_map/vtd,de->vte/dot_general | solution.py:20
  196.9 4.7 %fusion.24 = f32[12,196]{0,1:T(8,128)S(1)} fusion(f32[12,196,768]{2,1,0:T(8,128)S(1)} %fusion.44, bf16[12,196,768]{2,0,1:T(8,128)(2,1)} %all-gather.6.cloned.1.call-done), kind=kLoop, calls=%fused_computation.34 | loop fusion | flops 5416656 | bytes 10847424 | tf_op jit(solution)/shard_map/reduce_sum | solution.py:13
  201.6 7.0 %multiply_reduce_fusion.1 = f32[12,196]{0,1:T(8,128)S(1)} fusion(f32[12,196]{0,1:T(8,128)S(1)} %broadcast_multiply_fusion, f32[12,196,768]{2,1,0:T(8,128)S(1)} %fusion.44, bf16[12,196,768]{2,0,1:T(8,128)(2,1)} %all-gather.6.cloned.1.call-done), kind=kLoop, calls=%fused_computation.15 | loop fusion | flops 9029328 | bytes 10856832 | tf_op jit(solution)/shard_map/reduce_sum | solution.py:15
  208.7 5.1 %multiply_convert_fusion = bf16[12,196,768]{2,0,1:T(8,128)(2,1)} fusion(f32[768]{0:T(1024)S(1)} %copy-done.4, f32[12,196]{0,1:T(8,128)S(1)} %add_rsqrt_fusion, f32[12,196]{0,1:T(8,128)S(1)} %broadcast_multiply_fusion, f32[12,196,768]{2,1,0:T(8,128)S(1)} %fusion.44, bf16[12,196,768]{2,0,1:T(8,128)(2,1)S(1)} %bitcast.58), kind=kLoop, calls=%fused_computation.14 | loop fusion | flops 10838016 | bytes 14472576 | tf_op jit(solution)/shard_map/convert_element_type | solution.py:16
  213.9 6.7 %fusion.46 = f32[12,4,196]{2,1,0:T(4,128)S(1)} fusion(f32[512]{0:T(512)S(1)} %dynamic_slice.30, bf16[12,196,768]{2,0,1:T(8,128)(2,1)} %multiply_convert_fusion, bf16[768,1024]{1,0:T(8,128)(2,1)S(1)} %copy-done, s32[]{:T(128)S(6)} %select_n.36, bf16[4,1024]{1,0:T(4,128)(2,1)S(1)} %copy-done.9), kind=kOutput, calls=%fused_computation.49 | convolution fusion | flops 1871364096 | bytes 4443904 | tf_op jit(solution)/shard_map/vth,ch->vct/dot_general | solution.py:109
  220.6 3.7 %psum.7 = f32[12,4,196]{2,1,0:T(4,128)S(1)} all-reduce(f32[12,4,196]{2,1,0:T(4,128)S(1)} %fusion.46), channel_id=1, replica_groups=mesh['groups'=2,'pairs'=8,'mp'=2] {'mp'}, use_global_device_ids=true, to_apply=%region_8.0 | all-reduce | flops 9408 | bytes 75264 | tf_op jit(solution)/shard_map/psum | solution.py:110
  226.7 89.4 %all-reduce.3.cloned.1.call-done = f32[32,4,196]{2,1,0:T(4,128)} async-done(((f32[32,4,196]{2,1,0:T(4,128)}), f32[32,4,196]{2,1,0:T(4,128)}) %all-reduce.3.cloned.1.call-update) | async-done | bytes 100368
  (68 shorter events, 15.3 us)
Async XLA Ops:
  6.5 207.3 %copy-start = (bf16[768,1024]{1,0:T(8,128)(2,1)S(1)}, bf16[768,1024]{1,0:T(8,128)(2,1)}, u32[]{:S(2)}) copy-start(bf16[768,1024]{1,0:T(8,128)(2,1)} %param.22) | copy-start | bytes 4718596
  6.5 85.5 %all-gather.4.cloned.1.call-start = ((), (), s32[]{:S(2)}) async-start(), calls=%async_computation | async-start | bytes 5529600 | tf_op jit(solution)/shard_map/all_gather | solution.py:80
  8.7 102.1 %all-gather.6.cloned.1.call-start = ((), (), s32[]{:S(2)}) async-start(), calls=%async_computation.1 | async-start | bytes 7225344 | tf_op jit(solution)/shard_map/all_gather | solution.py:86
  96.8 94.9 %all-gather.8.cloned.1.call-start = ((), (), s32[]{:S(2)}) async-start(), calls=%async_computation.2 | async-start | bytes 5529600 | tf_op jit(solution)/shard_map/all_gather | solution.py:102
  114.3 1.8 copy-start.1
  117.5 8.1 %copy-start.2 = (f32[768]{0:T(1024)S(1)}, f32[768]{0:T(1024)}, u32[]{:S(2)}) copy-start(f32[768]{0:T(1024)} %param.16) | copy-start | bytes 9220
  128.3 3.3 %copy-start.6 = (bf16[768,768]{1,0:T(8,128)(2,1)S(1)}, bf16[768,768]{1,0:T(8,128)(2,1)}, u32[]{:S(2)}) copy-start(bf16[768,768]{1,0:T(8,128)(2,1)} %param.19) | copy-start | bytes 3538948
  135.1 6.5 %copy-start.3 = (f32[768]{0:T(1024)S(1)}, f32[768]{0:T(1024)}, u32[]{:S(2)}) copy-start(f32[768]{0:T(1024)} %param.15) | copy-start | bytes 9220
  141.6 4.3 %copy-start.7 = (bf16[768,768]{1,0:T(8,128)(2,1)S(1)}, bf16[768,768]{1,0:T(8,128)(2,1)}, u32[]{:S(2)}) copy-start(bf16[768,768]{1,0:T(8,128)(2,1)} %param.17) | copy-start | bytes 3538948
  173.3 4.3 %copy-start.10 = (s32[8]{0:T(128)S(1)}, s32[8]{0:T(128)}, u32[]{:S(2)}) copy-start(s32[8]{0:T(128)} %param.27) | copy-start | bytes 100
  173.3 5.5 %copy-start.5 = (f32[1024]{0:T(1024)S(1)}, f32[1024]{0:T(1024)}, u32[]{:S(2)}) copy-start(f32[1024]{0:T(1024)} %param.23) | copy-start | bytes 12292
  173.3 18.4 %copy-start.8 = (bf16[768,768]{1,0:T(8,128)(2,1)S(1)}, bf16[768,768]{1,0:T(8,128)(2,1)}, u32[]{:S(2)}) copy-start(bf16[768,768]{1,0:T(8,128)(2,1)} %param.20) | copy-start | bytes 3538948
  177.5 138.6 %all-reduce.3.cloned.1.call-start = ((), (), s32[]{:S(2)}) async-start(), calls=%async_computation.3 | async-start | bytes 262144
  196.9 11.8 %slice-start = ((s8[4816896]{0:T(1024)(128)(4,1)}), s8[622592]{0:T(1024)(128)(4,1)S(1)}, s32[]{:S(2)}) async-start(s8[4816896]{0:T(1024)(128)(4,1)} %bitcast.57), calls=%async_computation.4 | async-start | bytes 1245184
  201.6 7.1 %slice-start.1 = ((s8[4816896]{0:T(1024)(128)(4,1)}), s8[4194304]{0:T(1024)(128)(4,1)S(1)}, s32[]{:S(2)}) async-start(s8[4816896]{0:T(1024)(128)(4,1)} %bitcast.57), calls=%async_computation.5 | async-start | bytes 8388608
  201.6 7.1 %copy-start.4 = (f32[768]{0:T(1024)S(1)}, f32[768]{0:T(1024)}, u32[]{:S(2)}) copy-start(f32[768]{0:T(1024)} %param.21) | copy-start | bytes 9220
  208.7 5.2 %copy-start.9 = (bf16[4,1024]{1,0:T(4,128)(2,1)S(1)}, bf16[4,1024]{1,0:T(4,128)(2,1)}, u32[]{:S(2)}) copy-start(bf16[4,1024]{1,0:T(4,128)(2,1)} %param.24) | copy-start | bytes 24580
  213.9 11.6 %copy-start.11 = (u32[32]{0:T(128)S(1)}, u32[32]{0:T(128)}, u32[]{:S(2)}) copy-start(u32[32]{0:T(128)} %constant.82) | copy-start | bytes 388
Sparse Core Ops, SparseCore 0:
  9.5 82.4 all-gather.3
  96.9 13.8 all-gather.5
  177.6 14.0 all-gather.7
  225.6 90.4 all-reduce.2
where the time goes:
time: 325 us; the launch traced here: 324 us
  waiting for transfers between devices  197 us (61%)
  matrix products  48.5 us (15%)
  other arithmetic  35.4 us (11%)
  local copies, waits for them, and re-layouts  24.9 us (8%)
  between operations  14.1 us (4%)
  blocking collectives  3.65 us (1%)
    unnamed x5, waiting for transfers between devices  89.4 us
    all_gather x1, waiting for transfers between devices, per_device(): shard_rows = lax.all_gather(tokens, 'pairs', axis=0, tiled=True)  81.8 us
    dot_general x4, matrix products, project(): jnp.einsum('vtd,de->vte', rows_in, weight, preferred_element_type=jnp.flo...  14.9 us
    all_gather x1, waiting for transfers between devices, per_device(): full_views = lax.all_gather(half_views, 'mp', axis=2, tiled=True)  14 us
    sub x1, matrix products, attention(): exponent = jnp.exp(scores - row_max)  13 us
    reduce_sum x3, other arithmetic, norm_rows(): variance = jnp.mean(centered * centered, axis=-1, keepdims=True)  12.5 us
    convert_element_type x3, other arithmetic, norm_rows(): (centered * lax.rsqrt(variance + EPS) * gain_vec).astype(jnp.bfloat16)  12.2 us
    all_gather x1, waiting for transfers between devices, per_device(): attended = lax.all_gather(attended_part, 'mp', axis=2, tiled=True)  12.1 us
  transfers between devices with their start and end apart: 4, of which 4 were waited for; matrix products, arithmetic and copies ran while one was open for 1% of the time, Pallas kernels for 0%

commit v1 on v0

--- a/solution.py
+++ b/solution.py
@@ -77,7 +77,23 @@
     local_rows = view_local.reshape(worker_count, request_count)
     global_rows = owners * image_count + local_rows
     my_images = global_rows[worker_index]
-    shard_rows = lax.all_gather(tokens, "pairs", axis=0, tiled=True)
+    parts_out = lax.axis_size("pairs")
+    e_next = lax.axis_index("pairs")
+    found_now, x_now, val2 = (parts_out, e_next, tokens.shape[0])
+    log = [src_i * found_now if k == 0 else src_i for k, src_i in enumerate(tokens.shape)]
+    fresh = jnp.zeros(log, tokens.dtype)
+    shard_rows = lax.dynamic_update_slice_in_dim(fresh, tokens, x_now * val2, axis=0)
+    before = val = tokens
+    for hop_no in range(1, found_now // 2 + 1):
+        before = lax.ppermute(before, "pairs", [(k, (k + 1) % found_now) for k in range(found_now)])
+        shard_rows = lax.dynamic_update_slice_in_dim(
+            shard_rows, before, (x_now - hop_no) % found_now * val2, axis=0
+        )
+        if 2 * hop_no < found_now:
+            val = lax.ppermute(val, "pairs", [(k, (k - 1) % found_now) for k in range(found_now)])
+            shard_rows = lax.dynamic_update_slice_in_dim(
+                shard_rows, val, (x_now + hop_no) % found_now * val2, axis=0
+            )
     row_ids = jnp.arange(shard_rows.shape[0])
     onehot = (my_images[:, None] == row_ids[None, :]).astype(jnp.bfloat16)
     half_views = jnp.einsum(

time: 325 us -> 341 us (1.049); the launches traced: 324 us -> 335 us
  starting transfers between devices: 0.13 us -> 11.3 us
  local copies, waits for them, and re-layouts: 24.9 us -> 28.8 us
    all_gather x1 -> x0, waiting for transfers between devices: 81.8 us -> none  [per_device(): shard_rows = lax.all_gather(tokens, 'pairs', axis=0, tiled=True)]
    ppermute x0 -> x7, waiting for transfers between devices: none -> 77.3 us  [the longest x4 77.3 us: per_device(): lax.ppermute(before, 'pairs', [(k, (k + 1) % found_now) for k in range(fo...]
    ppermute x0 -> x7, starting transfers between devices: none -> 11.2 us  [the longest x4 8.86 us: per_device(): lax.ppermute(before, 'pairs', [(k, (k + 1) % found_now) for k in range(fo...]
    dynamic_update_slice x0 -> x8, local copies, waits for them, and re-layouts: none -> 5.48 us  [the longest x4 2.74 us: per_device(): lax.dynamic_update_slice_in_dim(shard_rows, before, (x_now - hop_no) % fo...]
    unnamed x5 -> x4, waiting for transfers between devices: 89.4 us -> 89.3 us
  transfers between devices with their start and end apart: 4 -> 10, of which waited for: 4 -> 7; matrix products, arithmetic and copies ran while one was open for 1% -> 3% of each run, Pallas kernels for 0% -> 0%
where the time goes in v1:
time: 341 us; the launch traced here: 335 us
  waiting for transfers between devices  195 us (57%)
  matrix products  46.1 us (14%)
  other arithmetic  35.7 us (10%)
  local copies, waits for them, and re-layouts  28.8 us (8%)
  between operations  14.4 us (4%)
  starting transfers between devices  11.3 us (3%)
  blocking collectives  3.65 us (1%)
    unnamed x4, waiting for transfers between devices  89.3 us
    ppermute x4, waiting for transfers between devices, per_device(): lax.ppermute(before, 'pairs', [(k, (k + 1) % found_now) for k in range(fo...  77.3 us
    all_gather x1, waiting for transfers between devices, per_device(): full_views = lax.all_gather(half_views, 'mp', axis=2, tiled=True)  15.8 us
    dot_general x4, matrix products, project(): jnp.einsum('vtd,de->vte', rows_in, weight, preferred_element_type=jnp.flo...  14.9 us
    sub x1, matrix products, attention(): exponent = jnp.exp(scores - row_max)  13 us
    reduce_sum x3, other arithmetic, norm_rows(): variance = jnp.mean(centered * centered, axis=-1, keepdims=True)  12.9 us
    convert_element_type x3, other arithmetic, norm_rows(): (centered * lax.rsqrt(variance + EPS) * gain_vec).astype(jnp.bfloat16)  12.2 us
    all_gather x1, waiting for transfers between devices, per_device(): attended = lax.all_gather(attended_part, 'mp', axis=2, tiled=True)  12.1 us
  transfers between devices with their start and end apart: 10, of which 7 were waited for; matrix products, arithmetic and copies ran while one was open for 3% of the time, Pallas kernels for 0%

profile of v1, /device:TPU:8, one launch (start us, length us, event | category | flops | bytes accessed | tf_op | source)
XLA Modules:
  0.0 334.6 jit_solution(3713429233908504908)
XLA Ops:
  9.5 24.7 %collective-permute-done = bf16[4,196,384]{2,0,1:T(4,128)(2,1)S(1)} collective-permute-done((bf16[4,196,384]{2,0,1:T(4,128)(2,1)}, bf16[4,196,384]{2,0,1:T(4,128)(2,1)S(1)}, u32[]{:S(2)}, u32[]{:S(2)}) %collective-permute-start) | collective-permute-done | bytes 602144 | tf_op jit(solution)/shard_map/ppermute | solution.py:88
  37.1 24.3 %collective-permute-done.2 = bf16[4,196,384]{2,0,1:T(4,128)(2,1)} collective-permute-done((bf16[4,196,384]{2,0,1:T(4,128)(2,1)S(1)}, bf16[4,196,384]{2,0,1:T(4,128)(2,1)}, u32[]{:S(2)}, u32[]{:S(2)}) %collective-permute-start.2) | collective-permute-done | bytes 602144 | tf_op jit(solution)/shard_map/ppermute | solution.py:88
  67.2 21.3 %collective-permute-done.4 = bf16[4,196,384]{2,0,1:T(4,128)(2,1)S(1)} collective-permute-done((bf16[4,196,384]{2,0,1:T(4,128)(2,1)}, bf16[4,196,384]{2,0,1:T(4,128)(2,1)S(1)}, u32[]{:S(2)}, u32[]{:S(2)}) %collective-permute-start.4) | collective-permute-done | bytes 602144 | tf_op jit(solution)/shard_map/ppermute | solution.py:88
  95.1 7.0 %collective-permute-done.6 = bf16[4,196,384]{2,0,1:T(4,128)(2,1)S(1)} collective-permute-done((bf16[4,196,384]{2,0,1:T(4,128)(2,1)S(1)}, bf16[4,196,384]{2,0,1:T(4,128)(2,1)S(1)}, u32[]{:S(2)}, u32[]{:S(2)}) %collective-permute-start.6) | collective-permute-done | bytes 602144 | tf_op jit(solution)/shard_map/ppermute | solution.py:88
  104.9 15.8 %all-gather.3.cloned.1.call-done = bf16[12,196,768]{2,0,1:T(8,128)(2,1)} async-done(((bf16[12,196,384]{2,0,1:T(8,128)(2,1)}), bf16[12,196,768]{2,0,1:T(8,128)(2,1)}) %all-gather.3.cloned.1.call-update) | async-done | bytes 3612688 | tf_op jit(solution)/shard_map/all_gather | solution.py:102
  120.8 3.5 %copy.39 = bf16[12,196,768]{2,1,0:T(8,128)(2,1)S(1)} copy(bf16[12,196,768]{2,0,1:T(8,128)(2,1)} %all-gather.3.cloned.1.call-done) | data formatting | bytes 7225344 | tf_op jit(solution)/shard_map/all_gather | solution.py:102
  127.9 3.2 convert_reduce_fusion
  131.2 4.1 %fusion.6 = f32[12,196]{0,1:T(8,128)S(1)} fusion(bf16[12,196,768]{2,0,1:T(8,128)(2,1)} %all-gather.3.cloned.1.call-done, f32[12,196]{0,1:T(8,128)S(1)} %broadcast_multiply_fusion.1), kind=kLoop, calls=%fused_computation.11 | loop fusion | flops 7222992 | bytes 3631488 | tf_op jit(solution)/shard_map/reduce_sum | solution.py:15
  138.8 3.3 convolution_convert_fusion.1
  142.1 3.4 %convolution_convert_fusion.2 = bf16[12,196,384]{2,1,0:T(8,128)(2,1)} fusion(bf16[12,196,768]{2,1,0:T(8,128)(2,1)S(1)} %fusion.11, bf16[768,768]{1,0:T(8,128)(2,1)S(1)} %copy-done.9, s32[]{:T(128)S(6)} %select_n.106), kind=kOutput, calls=%fused_computation.43 | convolution fusion | flops 1388169216 | bytes 6082564 | tf_op jit(solution)/shard_map/vtd,de->vte/dot_general | solution.py:20
  145.6 4.0 %copy.40 = bf16[12,196,384]{1,2,0:T(8,128)(2,1)} copy(bf16[12,196,384]{2,1,0:T(8,128)(2,1)} %convolution_convert_fusion.2) | data formatting | bytes 3612672 | tf_op jit(solution)/shard_map/convert_element_type | solution.py:116
  152.1 4.3 %fusion.8 = bf16[12,196,768]{2,0,1:T(8,128)(2,1)S(1)} fusion(bf16[12,196,768]{2,0,1:T(8,128)(2,1)} %all-gather.3.cloned.1.call-done, f32[768]{0:T(1024)S(1)} %copy-done.6, f32[12,196]{0,1:T(8,128)} %add_rsqrt_fusion.1, f32[12,196]{0,1:T(8,128)S(1)} %broadcast_multiply_fusion.1), kind=kLoop, calls=%fused_computation.13 | loop fusion | flops 9031680 | bytes 7247232 | tf_op jit(solution)/shard_map/convert_element_type | solution.py:16
  156.4 2.9 fusion.30
  162.0 13.0 %fusion.78 = (f32[12,6,196]{2,1,0:T(8,128)S(1)}, f32[12,6,196,196]{2,3,1,0:T(8,128)}) fusion(bf16[12,196,6,64]{1,3,2,0:T(8,128)(2,1)} %bitcast.65, bf16[12,196,6,64]{1,3,2,0:T(8,128)(2,1)} %bitcast.64), kind=kOutput, calls=%fused_computation.104 | convolution fusion | flops 362339904 | bytes 14732928 | tf_op jit(solution)/shard_map/sub | solution.py:34
  174.9 9.0 %fusion.29 = bf16[12,6,64,196]{3,2,1,0:T(8,128)(2,1)} fusion(bf16[12,196,6,64]{1,3,2,0:T(8,128)(2,1)} %bitcast.63, f32[12,6,196,196]{2,3,1,0:T(8,128)} %get-tuple-element.6, f32[12,6,196]{2,1,0:T(8,128)S(1)} %get-tuple-element.5), kind=kOutput, calls=%fused_computation.40 | convolution fusion | flops 360476928 | bytes 14732928 | tf_op jit(solution)/shard_map/vhqk,vkhd->vqhd/dot_general | solution.py:36
  183.9 4.2 %copy.45 = bf16[12,196,384]{2,1,0:T(8,128)(2,1)} copy(bf16[12,196,384]{1,2,0:T(8,128)(2,1)} %bitcast.66) | data formatting | bytes 3612672 | tf_op jit(solution)/shard_map/reshape | solution.py:42
  190.2 12.1 %all-gather.5.cloned.1.call-done = bf16[12,196,768]{2,1,0:T(8,128)(2,1)} async-done(((bf16[12,196,384]{2,1,0:T(8,128)(2,1)}), bf16[12,196,768]{2,1,0:T(8,128)(2,1)}) %all-gather.5.cloned.1.call-update) | async-done | bytes 3612688 | tf_op jit(solution)/shard_map/all_gather | solution.py:118
  202.3 5.2 %fusion.39 = f32[12,196,768]{2,1,0:T(8,128)S(1)} fusion(bf16[12,196,768]{2,1,0:T(8,128)(2,1)} %all-gather.5.cloned.1.call-done, bf16[768,768]{1,0:T(8,128)(2,1)S(1)} %copy-done.11), kind=kOutput, calls=%fused_computation.45 | convolution fusion | flops 2774532096 | bytes 12017664 | tf_op jit(solution)/shard_map/vtd,de->vte/dot_general | solution.py:20
  207.5 4.7 %fusion.22 = f32[12,196]{0,1:T(8,128)S(1)} fusion(f32[12,196,768]{2,1,0:T(8,128)S(1)} %fusion.39, bf16[12,196,768]{2,0,1:T(8,128)(2,1)} %all-gather.3.cloned.1.call-done), kind=kLoop, calls=%fused_computation.32 | loop fusion | flops 5416656 | bytes 10847424 | tf_op jit(solution)/shard_map/reduce_sum | solution.py:13
  212.3 6.9 %multiply_reduce_fusion.1 = f32[12,196]{0,1:T(8,128)S(1)} fusion(f32[12,196]{0,1:T(8,128)S(1)} %broadcast_multiply_fusion, f32[12,196,768]{2,1,0:T(8,128)S(1)} %fusion.39, bf16[12,196,768]{2,0,1:T(8,128)(2,1)} %all-gather.3.cloned.1.call-done), kind=kLoop, calls=%fused_computation.15 | loop fusion | flops 9029328 | bytes 10856832 | tf_op jit(solution)/shard_map/reduce_sum | solution.py:15
  219.3 5.1 %multiply_convert_fusion = bf16[12,196,768]{2,0,1:T(8,128)(2,1)} fusion(f32[768]{0:T(1024)S(1)} %copy-done.7, f32[12,196]{0,1:T(8,128)S(1)} %add_rsqrt_fusion, f32[12,196]{0,1:T(8,128)S(1)} %broadcast_multiply_fusion, f32[12,196,768]{2,1,0:T(8,128)S(1)} %fusion.39, bf16[12,196,768]{2,0,1:T(8,128)(2,1)S(1)} %bitcast.59), kind=kLoop, calls=%fused_computation.14 | loop fusion | flops 10838016 | bytes 14472576 | tf_op jit(solution)/shard_map/convert_element_type | solution.py:16
  224.4 6.7 %fusion.41 = f32[12,4,196]{2,1,0:T(4,128)S(1)} fusion(f32[512]{0:T(512)S(1)} %dynamic_slice.30, bf16[12,196,768]{2,0,1:T(8,128)(2,1)} %multiply_convert_fusion, bf16[768,1024]{1,0:T(8,128)(2,1)S(1)} %copy-done, s32[]{:T(128)S(6)} %select_n.90, bf16[4,1024]{1,0:T(4,128)(2,1)S(1)} %copy-done.12), kind=kOutput, calls=%fused_computation.47 | convolution fusion | flops 1871364096 | bytes 4443904 | tf_op jit(solution)/shard_map/vth,ch->vct/dot_general | solution.py:125
  231.1 3.6 %psum.7 = f32[12,4,196]{2,1,0:T(4,128)S(1)} all-reduce(f32[12,4,196]{2,1,0:T(4,128)S(1)} %fusion.41), channel_id=1, replica_groups=mesh['groups'=2,'pairs'=8,'mp'=2] {'mp'}, use_global_device_ids=true, to_apply=%region_8.9 | all-reduce | flops 9408 | bytes 75264 | tf_op jit(solution)/shard_map/psum | solution.py:126
  237.2 89.3 %all-reduce.3.cloned.1.call-done = f32[32,4,196]{2,1,0:T(4,128)} async-done(((f32[32,4,196]{2,1,0:T(4,128)}), f32[32,4,196]{2,1,0:T(4,128)}) %all-reduce.3.cloned.1.call-update) | async-done | bytes 100368
  (93 shorter events, 38.4 us)
Async XLA Ops:
  6.5 217.9 %copy-start = (bf16[768,1024]{1,0:T(8,128)(2,1)S(1)}, bf16[768,1024]{1,0:T(8,128)(2,1)}, u32[]{:S(2)}) copy-start(bf16[768,1024]{1,0:T(8,128)(2,1)} %param.22) | copy-start | bytes 4718596
  6.5 59.4 %copy-start.2 = (bf16[4,196,384]{2,0,1:T(4,128)(2,1)S(1)}, bf16[4,196,384]{2,0,1:T(4,128)(2,1)}, u32[]{:S(2)}) copy-start(bf16[4,196,384]{2,0,1:T(4,128)(2,1)} %param.14) | copy-start | bytes 1806340
  6.5 114.2 %all-gather.3.cloned.1.call-start = ((), (), s32[]{:S(2)}) async-start(), calls=%async_computation | async-start | bytes 7225344 | tf_op jit(solution)/shard_map/all_gather | solution.py:102
  6.5 27.6 %collective-permute-start = (bf16[4,196,384]{2,0,1:T(4,128)(2,1)}, bf16[4,196,384]{2,0,1:T(4,128)(2,1)S(1)}, u32[]{:S(2)}, u32[]{:S(2)}) collective-permute-start(bf16[4,196,384]{2,0,1:T(4,128)(2,1)} %param.14), channel_id=1, source_target_pairs={{0,2},{2,4},{4,6},{6,8},{8,10},{10,12},{12,14},{14,0},{1,3},{3,5},... | collective-permute-start | bytes 1806344 | tf_op jit(solution)/shard_map/ppermute | solution.py:88
  8.1 28.4 %collective-permute-start.1 = (bf16[4,196,384]{2,0,1:T(4,128)(2,1)}, bf16[4,196,384]{2,0,1:T(4,128)(2,1)S(1)}, u32[]{:S(2)}, u32[]{:S(2)}) collective-permute-start(bf16[4,196,384]{2,0,1:T(4,128)(2,1)} %param.14), channel_id=1, source_target_pairs={{0,14},{2,0},{4,2},{6,4},{8,6},{10,8},{12,10},{14,12},{1,15},{3,1}... | collective-permute-start | bytes 1806344 | tf_op jit(solution)/shard_map/ppermute | solution.py:93
  34.1 27.3 %collective-permute-start.2 = (bf16[4,196,384]{2,0,1:T(4,128)(2,1)S(1)}, bf16[4,196,384]{2,0,1:T(4,128)(2,1)}, u32[]{:S(2)}, u32[]{:S(2)}) collective-permute-start(bf16[4,196,384]{2,0,1:T(4,128)(2,1)S(1)} %collective-permute-done), channel_id=1, source_target_pairs={{0,2},{2,4},{4,6},{6,8},{8,10},{10,12},{12,14},{14,0},{1,3},{3,5},... | collective-permute-start | bytes 1806344 | tf_op jit(solution)/shard_map/ppermute | solution.py:88
  36.5 29.8 %collective-permute-start.3 = (bf16[4,196,384]{2,0,1:T(4,128)(2,1)S(1)}, bf16[4,196,384]{2,0,1:T(4,128)(2,1)}, u32[]{:S(2)}, u32[]{:S(2)}) collective-permute-start(bf16[4,196,384]{2,0,1:T(4,128)(2,1)S(1)} %collective-permute-done.1), channel_id=1, source_target_pairs={{0,14},{2,0},{4,2},{6,4},{8,6},{10,8},{12,10},{14,12},{1,15},{3,1}... | collective-permute-start | bytes 1806344 | tf_op jit(solution)/shard_map/ppermute | solution.py:93
  61.4 27.1 %collective-permute-start.4 = (bf16[4,196,384]{2,0,1:T(4,128)(2,1)}, bf16[4,196,384]{2,0,1:T(4,128)(2,1)S(1)}, u32[]{:S(2)}, u32[]{:S(2)}) collective-permute-start(bf16[4,196,384]{2,0,1:T(4,128)(2,1)} %collective-permute-done.2), channel_id=1, source_target_pairs={{0,2},{2,4},{4,6},{6,8},{8,10},{10,12},{12,14},{14,0},{1,3},{3,5},... | collective-permute-start | bytes 1806344 | tf_op jit(solution)/shard_map/ppermute | solution.py:88
  66.4 28.3 %collective-permute-start.5 = (bf16[4,196,384]{2,0,1:T(4,128)(2,1)}, bf16[4,196,384]{2,0,1:T(4,128)(2,1)S(1)}, u32[]{:S(2)}, u32[]{:S(2)}) collective-permute-start(bf16[4,196,384]{2,0,1:T(4,128)(2,1)} %collective-permute-done.3), channel_id=1, source_target_pairs={{0,14},{2,0},{4,2},{6,4},{8,6},{10,8},{12,10},{14,12},{1,15},{3,1}... | collective-permute-start | bytes 1806344 | tf_op jit(solution)/shard_map/ppermute | solution.py:93
  88.5 13.7 %collective-permute-start.6 = (bf16[4,196,384]{2,0,1:T(4,128)(2,1)S(1)}, bf16[4,196,384]{2,0,1:T(4,128)(2,1)S(1)}, u32[]{:S(2)}, u32[]{:S(2)}) collective-permute-start(bf16[4,196,384]{2,0,1:T(4,128)(2,1)S(1)} %collective-permute-done.4), channel_id=1, source_target_pairs={{0,2},{2,4},{4,6},{6,8},{8,10},{10,12},{12,14},{14,0},{1,3},{3,5},... | collective-permute-start | bytes 1806344 | tf_op jit(solution)/shard_map/ppermute | solution.py:88
  104.8 97.5 %all-gather.5.cloned.1.call-start = ((), (), s32[]{:S(2)}) async-start(), calls=%async_computation.1 | async-start | bytes 5529600 | tf_op jit(solution)/shard_map/all_gather | solution.py:118
  127.9 8.1 %copy-start.5 = (f32[768]{0:T(1024)S(1)}, f32[768]{0:T(1024)}, u32[]{:S(2)}) copy-start(f32[768]{0:T(1024)} %param.16) | copy-start | bytes 9220
  138.8 3.3 %copy-start.9 = (bf16[768,768]{1,0:T(8,128)(2,1)S(1)}, bf16[768,768]{1,0:T(8,128)(2,1)}, u32[]{:S(2)}) copy-start(bf16[768,768]{1,0:T(8,128)(2,1)} %param.19) | copy-start | bytes 3538948
  145.6 6.5 %copy-start.6 = (f32[768]{0:T(1024)S(1)}, f32[768]{0:T(1024)}, u32[]{:S(2)}) copy-start(f32[768]{0:T(1024)} %param.15) | copy-start | bytes 9220
  152.1 4.3 %copy-start.10 = (bf16[768,768]{1,0:T(8,128)(2,1)S(1)}, bf16[768,768]{1,0:T(8,128)(2,1)}, u32[]{:S(2)}) copy-start(bf16[768,768]{1,0:T(8,128)(2,1)} %param.17) | copy-start | bytes 3538948
  183.9 4.3 %copy-start.13 = (s32[8]{0:T(128)S(1)}, s32[8]{0:T(128)}, u32[]{:S(2)}) copy-start(s32[8]{0:T(128)} %param.27) | copy-start | bytes 100
  183.9 5.6 %copy-start.8 = (f32[1024]{0:T(1024)S(1)}, f32[1024]{0:T(1024)}, u32[]{:S(2)}) copy-start(f32[1024]{0:T(1024)} %param.23) | copy-start | bytes 12292
  183.9 18.4 %copy-start.11 = (bf16[768,768]{1,0:T(8,128)(2,1)S(1)}, bf16[768,768]{1,0:T(8,128)(2,1)}, u32[]{:S(2)}) copy-start(bf16[768,768]{1,0:T(8,128)(2,1)} %param.20) | copy-start | bytes 3538948
  188.1 138.4 %all-reduce.3.cloned.1.call-start = ((), (), s32[]{:S(2)}) async-start(), calls=%async_computation.2 | async-start | bytes 262144
  207.5 11.7 %slice-start = ((s8[4816896]{0:T(1024)(128)(4,1)}), s8[622592]{0:T(1024)(128)(4,1)S(1)}, s32[]{:S(2)}) async-start(s8[4816896]{0:T(1024)(128)(4,1)} %bitcast.58), calls=%async_computation.3 | async-start | bytes 1245184
  212.2 7.0 %slice-start.1 = ((s8[4816896]{0:T(1024)(128)(4,1)}), s8[4194304]{0:T(1024)(128)(4,1)S(1)}, s32[]{:S(2)}) async-start(s8[4816896]{0:T(1024)(128)(4,1)} %bitcast.58), calls=%async_computation.4 | async-start | bytes 8388608
  212.3 7.0 %copy-start.7 = (f32[768]{0:T(1024)S(1)}, f32[768]{0:T(1024)}, u32[]{:S(2)}) copy-start(f32[768]{0:T(1024)} %param.21) | copy-start | bytes 9220
  219.3 5.2 %copy-start.12 = (bf16[4,1024]{1,0:T(4,128)(2,1)S(1)}, bf16[4,1024]{1,0:T(4,128)(2,1)}, u32[]{:S(2)}) copy-start(bf16[4,1024]{1,0:T(4,128)(2,1)} %param.24) | copy-start | bytes 24580
  224.4 11.6 %copy-start.14 = (u32[32]{0:T(128)S(1)}, u32[32]{0:T(128)}, u32[]{:S(2)}) copy-start(u32[32]{0:T(128)} %constant.131) | copy-start | bytes 388
  (3 other events, 6.0 us)
Sparse Core Ops, SparseCore 0:
  105.0 15.7 all-gather.2
  188.3 14.0 all-gather.4
  236.1 90.3 all-reduce.2
